TPU v7x, 32 devices: a whole 2x2x4 slice. The times are simulated.
32 devices in a mesh: groups: 2 (over x), frames: 16 (over z, y, core).
Axes of the slice: x: 2, y: 2, z: 4, core: 2. Of those that a mesh axis runs over, the one named last changes fastest.
Arguments:
- video: float32 [4, 16, 256, 256], P('groups', 'frames'), parts along dimension 0, may hold values from -9 to 9
- clip_start: int32 [4], P('groups'), parts along dimension 0, may hold values from 0 to 7
- gain_space: float32 [256], replicated, may hold values from 0.1 to 1.9
- qkv_space: float32 [256, 768], replicated, may hold values from -0.375 to 0.375
- out_space: float32 [256, 256], replicated, may hold values from -0.375 to 0.375
- gain_time: float32 [256], replicated, may hold values from 0.1 to 1.9
- qkv_time: float32 [256, 768], replicated, may hold values from -0.375 to 0.375
- out_time: float32 [256, 256], replicated, may hold values from -0.375 to 0.375
- code_sums: float32 [8192, 256], P(('groups', 'frames')), parts along dimension 0, may hold values from -12 to 12
- code_counts: float32 [8192], P(('groups', 'frames')), parts along dimension 0, may hold values from 1 to 10
Outputs:
- latents: float32 [4, 16, 256, 256], P('groups', None, 'frames'), parts along dimension 0
- new_sums: float32 [8192, 256], P(('groups', 'frames')), parts along dimension 0
- new_counts: float32 [8192], P(('groups', 'frames')), parts along dimension 0
- new_codebook: float32 [8192, 256], P(('groups', 'frames')), parts along dimension 0
There are 2 independent parts, one for each index of `groups`. A program takes and returns all parts, laid end to end along the dimension named above; an argument that names none is the same for every part. Nothing has to cross between parts.
All inputs are finite; a program needn't handle non-finite values.
Results may differ from a plain program's by a relative error of at most 0.0003.
Values sent between devices are 32-bit elements; how exact they have to be, the bound alone decides.
A program may use at most 64 MiB of HBM per device.

v0:
```python
import jax
import jax.numpy as jnp
from jax import lax
from jax.sharding import PartitionSpec as P

HEADS = 4
ATTN_SCALE = 10.0
SOFTMAX_WARMTH = 0.05
DECAY_RATE = 0.9
EPSILON = 1e-06
TOP_PRECISION = lax.Precision.HIGHEST


def rms_norm(values, gain_vec):
    return values * lax.rsqrt(jnp.mean(values * values, -1, keepdims=True) + EPSILON) * gain_vec


def unit_vec(values):
    return values * lax.rsqrt(jnp.sum(values * values, -1, keepdims=True) + EPSILON)


def spatial_block(one_frame, gain_vec, w_qkv, w_out):
    width = one_frame.shape[-1]
    normed = rms_norm(one_frame, gain_vec)
    packed = jnp.dot(normed, w_qkv, precision=TOP_PRECISION)
    queries = unit_vec(packed[:, :width].reshape(-1, HEADS, width // HEADS))
    key_vecs = unit_vec(packed[:, width : 2 * width].reshape(-1, HEADS, width // HEADS))
    values = packed[:, 2 * width :].reshape(-1, HEADS, width // HEADS)
    scores = ATTN_SCALE * jnp.einsum("qhd,khd->hqk", queries, key_vecs, precision=TOP_PRECISION)
    assignment_weights = jnp.exp(scores)
    totals = jnp.sum(assignment_weights, -1).T[:, :, None]
    mixed = jnp.einsum("hqk,khd->qhd", assignment_weights, values, precision=TOP_PRECISION) / totals
    return one_frame + jnp.dot(mixed.reshape(-1, width), w_out, precision=TOP_PRECISION)


def time_block(spaced, clip_start, gain_vec, w_qkv, w_out):
    clips, frames, places, width = spaced.shape
    normed = rms_norm(spaced, gain_vec)
    packed = jnp.einsum("ctpd,de->ctpe", normed, w_qkv, precision=TOP_PRECISION)
    shape_heads = (clips, frames, places, HEADS, width // HEADS)
    queries = unit_vec(packed[..., :width].reshape(shape_heads))
    key_vecs = unit_vec(packed[..., width : 2 * width].reshape(shape_heads))
    values = packed[..., 2 * width :].reshape(shape_heads)
    scores = ATTN_SCALE * jnp.einsum(
        "ctphd,csphd->cphts", queries, key_vecs, precision=TOP_PRECISION
    )
    later = jnp.arange(frames, dtype=jnp.int32)[:, None]
    earlier = jnp.arange(frames, dtype=jnp.int32)[None, :]
    allowed = (earlier <= later)[None] & (
        (earlier[None] >= clip_start[:, None, None]) | (earlier == later)[None]
    )
    assignment_weights = jnp.exp(scores) * allowed[:, None, None, :, :].astype(jnp.float32)
    totals = jnp.transpose(jnp.sum(assignment_weights, -1), (0, 3, 1, 2))[..., None]
    mixed = (
        jnp.einsum("cphts,csphd->ctphd", assignment_weights, values, precision=TOP_PRECISION)
        / totals
    )
    return spaced + jnp.einsum(
        "ctpd,de->ctpe", mixed.reshape(clips, frames, places, width), w_out, precision=TOP_PRECISION
    )


def local(
    video,
    clip_start,
    gain_space,
    qkv_space,
    out_space,
    gain_time,
    qkv_time,
    out_time,
    code_sums,
    code_counts,
):
    clips, local_frames, places, width = video.shape
    flat_frames = video.reshape(clips * local_frames, places, width)
    spaced = lax.map(
        lambda one_frame: spatial_block(one_frame, gain_space, qkv_space, out_space), flat_frames
    )
    spaced = spaced.reshape(clips, local_frames, places, width)
    by_place = lax.all_to_all(spaced, "frames", split_axis=2, concat_axis=1, tiled=True)
    latents = time_block(by_place, clip_start, gain_time, qkv_time, out_time)
    unit_token_vectors = unit_vec(latents.reshape(-1, width))
    local_codes = unit_vec(code_sums / code_counts[:, None])
    codebook_matrix = lax.all_gather(local_codes, "frames", axis=0, tiled=True)
    assignment_weights = jnp.exp(
        jnp.dot(unit_token_vectors, codebook_matrix.T, precision=TOP_PRECISION) / SOFTMAX_WARMTH
    )
    probs = assignment_weights / jnp.sum(assignment_weights, 1, keepdims=True)
    term_sums = lax.dot_general(
        probs, unit_token_vectors, (((0,), (0,)), ((), ())), precision=TOP_PRECISION
    )
    term_counts = jnp.sum(probs, 0)
    got_sums, got_counts = (
        lax.psum_scatter(term_sums, "frames", scatter_dimension=0, tiled=True),
        lax.psum_scatter(term_counts, "frames", scatter_dimension=0, tiled=True),
    )
    new_sums = DECAY_RATE * code_sums + (1.0 - DECAY_RATE) * got_sums
    new_counts = DECAY_RATE * code_counts + (1.0 - DECAY_RATE) * got_counts
    new_codebook = new_sums / new_counts[:, None]
    return (latents, new_sums, new_counts, new_codebook)


def solution(mesh):
    in_specs = (
        P("groups", "frames", None, None),
        P("groups"),
        P(),
        P(),
        P(),
        P(),
        P(),
        P(),
        P(("groups", "frames"), None),
        P(("groups", "frames")),
    )
    out_specs = (
        P("groups", None, "frames", None),
        P(("groups", "frames"), None),
        P(("groups", "frames")),
        P(("groups", "frames"), None),
    )
    return jax.shard_map(local, mesh=mesh, in_specs=in_specs, out_specs=out_specs, check_vma=False)
```

profile of v0, /device:TPU:0, one launch (start us, length us, event | category | flops | bytes accessed | tf_op | source)
XLA Modules:
  0.0 198.9 jit_solution(9034979632726046601)
XLA Ops:
  7.2 1.2 multiply_reduce_fusion.6
  8.4 1.8 broadcast_multiply_fusion.2
  10.3 25.9 %while.10 = (s32[]{:T(128)}, f32[2,256,256]{2,0,1:T(2,128)}, f32[2,256,256]{2,1,0:T(8,128)}, f32[256]{0:T(256)}, f32[256,768]{1,0:T(8,128)}, /*index=5*/f32[256,256]{1,0:T(8,128)}, s32[]{:T(128)}, s32[]{:T(128)}) while((s32[]{:T(128)}, f32[2,256,256]{2,0,1:T(2,128)}, f32[2,256,256]{2,1,0:T(8,128)}, f32[256]{0:T(256)}, f32[256,768]{1,0:T(8,128)}, ...), condition=%wide.region_5.6_spmd, body=%wide.region_0.5_spmd.sunk | while | flops 1209269504 | bytes 14202521 | solution.py:77
  11.5 2.1 %fusion.68 = f32[256,768]{1,0:T(8,128)S(1)} fusion(f32[256,768]{1,0:T(8,128)} %get-tuple-element.142, f32[2,256,256]{2,1,0:T(8,128)} %get-tuple-element.140, s32[]{:T(128)} %get-tuple-element.130, f32[256]{0:T(256)} %get-tuple-element.141, f32[256]{0:T(256)S(1)} %add_rsqrt_fusion.10), kind=kOutput, calls=%fused_computation.10.clone.1 | convolution fusion | flops 604110848 | bytes 1837568 | tf_op jit(solution)/shard_map/while/body/eval_jaxpr/dot_general | solution.py:25
  16.9 6.3 %dynamic_update_slice.5 = f32[2,256,256]{2,0,1:T(2,128)} dynamic-update-slice(f32[2,256,256]{2,0,1:T(2,128)} %get-tuple-element.131, f32[1,256,256]{2,0,1:T(1,128)S(1)} %copy.85, s32[]{:T(128)} %get-tuple-element.130, s32[]{:T(128)} %constant.22.clone.1..sunk, s32[]{:T(128)} %constant.22.clone.1..sunk) | dynamic-update-slice | bytes 524292 | tf_op jit(solution)/shard_map/while/body/jit(dynamic_update_index_in_dim)/dynamic_update_slice | solution.py:77
  24.4 2.1 %fusion.68 = f32[256,768]{1,0:T(8,128)S(1)} fusion(f32[256,768]{1,0:T(8,128)} %get-tuple-element.142, f32[2,256,256]{2,1,0:T(8,128)} %get-tuple-element.140, s32[]{:T(128)} %get-tuple-element.130, f32[256]{0:T(256)} %get-tuple-element.141, f32[256]{0:T(256)S(1)} %add_rsqrt_fusion.10), kind=kOutput, calls=%fused_computation.10.clone.1 | convolution fusion | flops 604110848 | bytes 1837568 | tf_op jit(solution)/shard_map/while/body/eval_jaxpr/dot_general | solution.py:25
  29.9 6.3 %dynamic_update_slice.5 = f32[2,256,256]{2,0,1:T(2,128)} dynamic-update-slice(f32[2,256,256]{2,0,1:T(2,128)} %get-tuple-element.131, f32[1,256,256]{2,0,1:T(1,128)S(1)} %copy.85, s32[]{:T(128)} %get-tuple-element.130, s32[]{:T(128)} %constant.22.clone.1..sunk, s32[]{:T(128)} %constant.22.clone.1..sunk) | dynamic-update-slice | bytes 524292 | tf_op jit(solution)/shard_map/while/body/jit(dynamic_update_index_in_dim)/dynamic_update_slice | solution.py:77
  36.2 7.4 %all-to-all-start = ((f32[2,1,256,256]{3,0,1,2:T(2,128)}), f32[2,1,256,256]{3,0,1,2:T(2,128)S(1)}, u32[]{:S(2)}, u32[]{:S(2)}) async-start(f32[2,1,256,256]{3,0,1,2:T(2,128)} %bitcast.103), calls=%async_computation | async-start | bytes 1048576 | tf_op jit(solution)/shard_map/all_to_all | solution.py:81
  43.8 22.8 %all-to-all-done = f32[2,1,256,256]{3,0,1,2:T(2,128)S(1)} async-done(((f32[2,1,256,256]{3,0,1,2:T(2,128)}), f32[2,1,256,256]{3,0,1,2:T(2,128)S(1)}, u32[]{:S(2)}, u32[]{:S(2)}) %all-to-all-start) | async-done | bytes 524320 | tf_op jit(solution)/shard_map/all_to_all | solution.py:81
  67.3 1.5 fusion.23
  68.8 1.2 fusion.37
  70.4 1.5 reshape.171
  71.9 2.5 %reshape.170 = f32[2,16,16,4,64]{4,3,2,1,0:T(4,128)} reshape(f32[2,16,16,256]{3,2,1,0:T(8,128)} %get-tuple-element.58) | data formatting | bytes 1048576 | tf_op jit(solution)/shard_map/reshape | solution.py:43
  75.7 1.5 broadcast_multiply_fusion
  77.1 3.1 %fusion.38 = (f32[2,16,4,16]{3,2,1,0:T(4,128)S(1)}, f32[2,16,4,16,16]{3,4,2,1,0:T(8,128)S(1)}) fusion(f32[2,16,16]{1,2,0:T(8,128)S(1)} %and_convert_fusion, f32[2,16,16,4,64]{4,3,2,1,0:T(4,128)S(1)} %get-tuple-element.69, f32[2,16,16,4,64]{4,3,2,1,0:T(4,128)S(1)} %get-tuple-element.70), kind=kOutput, calls=%fused_computation.72 | convolution fusion | flops 25262080 | bytes 1189888 | tf_op jit(solution)/shard_map/ctphd,csphd->cphts/dot_general | solution.py:44
  80.3 2.5 %fusion.17 = f32[2,16,16,4,64]{4,1,3,2,0:T(8,128)S(1)} fusion(f32[2,16,4,16,16]{3,4,2,1,0:T(8,128)S(1)} %get-tuple-element.62, f32[2,16,16,4,64]{4,3,2,1,0:T(4,128)S(1)} %copy-done.6, f32[2,16,16,4]{1,3,2,0:T(4,128)S(1)} %bitcast.106), kind=kOutput, calls=%fused_computation.28 | convolution fusion | flops 25296896 | bytes 1187840 | tf_op jit(solution)/shard_map/cphts,csphd->ctphd/dot_general | solution.py:55
  83.9 1.6 multiply_reduce_fusion.4
  85.8 9.9 %fusion.16 = (f32[512]{0:T(512)S(1)}, f32[512,4096]{1,0:T(8,128)S(1)}) fusion(f32[512,256]{1,0:T(8,128)S(1)} %bitcast_multiply_fusion.2, f32[4096,256]{1,0:T(8,128)} %all-gather.2.cloned.1.call-done), kind=kOutput, calls=%fused_computation.26 | convolution fusion | flops 6446644736 | bytes 13109248 | tf_op jit(solution)/shard_map/dot_general | solution.py:87
  95.7 3.2 %copy-done.1 = f32[512,4096]{1,0:T(8,128)} copy-done((f32[512,4096]{1,0:T(8,128)}, f32[512,4096]{1,0:T(8,128)S(1)}, u32[]{:S(2)}) %copy-start.1) | copy-done | bytes 8388632
  98.9 15.0 %fusion.28 = f32[4096,256]{1,0:T(8,128)} fusion(f32[512,256]{1,0:T(8,128)S(1)} %bitcast_multiply_fusion.2, f32[512,4096]{1,0:T(8,128)S(1)} %get-tuple-element.66, f32[512]{0:T(512)S(1)} %get-tuple-element.65), kind=kOutput, calls=%fused_computation.48 | convolution fusion | flops 6446645248 | bytes 13109248 | tf_op jit(solution)/shard_map/dot_general | solution.py:90
  115.2 4.3 %fusion.27 = f32[4096]{0:T(1024)S(1)} fusion(f32[512]{0:T(512)S(1)} %get-tuple-element.65, f32[512,4096]{1,0:T(8,128)} %copy-done.1), kind=kLoop, calls=%fused_computation.47 | loop fusion | flops 6287360 | bytes 8407040 | tf_op jit(solution)/shard_map/reduce_sum | solution.py:93
  119.5 64.5 %all-reduce = f32[4096]{0:T(1024)S(1)} all-reduce(f32[4096]{0:T(1024)S(1)} %fusion.27), channel_id=3, replica_groups=mesh['groups'=2,'frames'=16] {'frames'}, use_global_device_ids=true, to_apply=%region_15.16.clone | all-reduce | flops 4096 | bytes 32768
  184.1 6.2 %reduce-scatter.2.cloned.1.call-done = f32[256,256]{1,0:T(8,128)} async-done(((f32[4096,256]{1,0:T(8,128)}), f32[256,256]{1,0:T(8,128)}) %reduce-scatter.2.cloned.1.call-update) | async-done | bytes 262160 | tf_op jit(solution)/shard_map/reduce_scatter | solution.py:95
  190.3 1.8 broadcast_divide_fusion
  (79 shorter events, 13.5 us)
Async XLA Ops:
  7.2 60.1 %copy-start = (f32[256,768]{1,0:T(8,128)S(1)}, f32[256,768]{1,0:T(8,128)}, u32[]{:S(2)}) copy-start(f32[256,768]{1,0:T(8,128)} %param.18) | copy-start | bytes 2359300
  7.2 78.6 %all-gather.2.cloned.1.call-start = ((), (), s32[]{:S(2)}) async-start(), calls=%async_computation.2 | async-start | bytes 4456448 | tf_op jit(solution)/shard_map/all_gather | solution.py:85
  10.3 33.4 %copy-start.10 = (s32[2]{0:T(128)S(1)}, s32[2]{0:T(128)}, u32[]{:S(2)}) copy-start(s32[2]{0:T(128)} %param.13) | copy-start | bytes 28
  10.3 57.0 %copy-start.9 = (f32[256]{0:T(256)S(1)}, f32[256]{0:T(256)}, u32[]{:S(2)}) copy-start(f32[256]{0:T(256)} %param.17) | copy-start | bytes 3076
  10.3 5.7 %copy-start.2 = (f32[2,256,256]{2,1,0:T(8,128)S(1)}, f32[2,256,256]{2,1,0:T(8,128)}, u32[]{:S(2)}) copy-start(f32[2,256,256]{2,1,0:T(8,128)} %get-tuple-element.140) | copy-start | bytes 1572868 | tf_op jit(solution)/shard_map/while
  10.3 5.7 %copy-start.3 = (f32[256,256]{1,0:T(8,128)S(1)}, f32[256,256]{1,0:T(8,128)}, u32[]{:S(2)}) copy-start(f32[256,256]{1,0:T(8,128)} %get-tuple-element.143) | copy-start | bytes 786436 | tf_op jit(solution)/shard_map/while
  23.3 5.7 %copy-start.2 = (f32[2,256,256]{2,1,0:T(8,128)S(1)}, f32[2,256,256]{2,1,0:T(8,128)}, u32[]{:S(2)}) copy-start(f32[2,256,256]{2,1,0:T(8,128)} %get-tuple-element.140) | copy-start | bytes 1572868 | tf_op jit(solution)/shard_map/while
  23.3 5.7 %copy-start.3 = (f32[256,256]{1,0:T(8,128)S(1)}, f32[256,256]{1,0:T(8,128)}, u32[]{:S(2)}) copy-start(f32[256,256]{1,0:T(8,128)} %get-tuple-element.143) | copy-start | bytes 786436 | tf_op jit(solution)/shard_map/while
  36.2 30.5 %all-to-all-start = ((f32[2,1,256,256]{3,0,1,2:T(2,128)}), f32[2,1,256,256]{3,0,1,2:T(2,128)S(1)}, u32[]{:S(2)}, u32[]{:S(2)}) async-start(f32[2,1,256,256]{3,0,1,2:T(2,128)} %bitcast.103), calls=%async_computation | async-start | bytes 1048576 | tf_op jit(solution)/shard_map/all_to_all | solution.py:81
  43.6 146.7 %reduce-scatter.2.cloned.1.call-start = ((), (), s32[]{:S(2)}) async-start(), calls=%async_computation.3 | async-start | bytes 4456448 | tf_op jit(solution)/shard_map/reduce_scatter | solution.py:95
  74.3 6.0 %copy-start.6 = (f32[2,16,16,4,64]{4,3,2,1,0:T(4,128)S(1)}, f32[2,16,16,4,64]{4,3,2,1,0:T(4,128)}, u32[]{:S(2)}) copy-start(f32[2,16,16,4,64]{4,3,2,1,0:T(4,128)} %reshape.170) | copy-start | bytes 1572868
  85.5 28.5 %copy-start.5 = (f32[2,16,16,256]{3,2,1,0:T(8,128)}, f32[2,16,16,256]{3,2,1,0:T(8,128)S(1)}, u32[]{:S(2)}) copy-start(f32[2,16,16,256]{3,2,1,0:T(8,128)S(1)} %get-tuple-element.64) | copy-start | bytes 1572868
  95.7 3.2 %copy-start.1 = (f32[512,4096]{1,0:T(8,128)}, f32[512,4096]{1,0:T(8,128)S(1)}, u32[]{:S(2)}) copy-start(f32[512,4096]{1,0:T(8,128)S(1)} %get-tuple-element.66) | copy-start | bytes 25165828
  98.9 15.1 %copy-start.11 = (u32[32]{0:T(128)S(1)}, u32[32]{0:T(128)}, u32[]{:S(2)}) copy-start(u32[32]{0:T(128)} %constant.46) | copy-start | bytes 388
  114.0 70.1 %copy-start.7 = (f32[256]{0:T(256)S(1)}, f32[256]{0:T(256)}, u32[]{:S(2)}) copy-start(f32[256]{0:T(256)} %param.21) | copy-start | bytes 3076
  114.0 76.3 %copy-start.4 = (f32[256,256]{1,0:T(8,128)S(1)}, f32[256,256]{1,0:T(8,128)}, u32[]{:S(2)}) copy-start(f32[256,256]{1,0:T(8,128)} %param.20) | copy-start | bytes 786436
  184.1 8.0 %copy-start.8 = (f32[256]{0:T(256)}, f32[256]{0:T(256)S(1)}, u32[]{:S(2)}) copy-start(f32[256]{0:T(256)S(1)} %fusion.33) | copy-start | bytes 3076
Sparse Core Ops, SparseCore 0:
  10.7 62.2 all-gather.1
  114.1 76.1 reduce-scatter.1
where the time goes:
time: 200 us; the launch traced here: 199 us
  blocking collectives  64.5 us (32%)
  matrix products  42.9 us (21%)
  waiting for transfers between devices  29.1 us (15%)
  local copies, waits for them, and re-layouts  24.8 us (12%)
  other arithmetic  15 us (8%)
  between operations  14.9 us (7%)
  starting transfers between devices  7.5 us (4%)
    unnamed x1, blocking collectives  64.5 us
    all_to_all x1, waiting for transfers between devices, local(): lax.all_to_all(spaced, 'frames', split_axis=2, concat_axis=1, tiled=True)  22.8 us
    dot_general x1, matrix products, local(): lax.dot_general(probs, unit_token_vectors, (((0,), (0,)), ((), ())), prec...  15 us
    dynamic_update_slice x4, local copies, waits for them, and re-layouts, local(): lax.map(lambda one_frame: spatial_block(one_frame, gain_space, qkv_space,...  13.2 us
    dot_general x1, matrix products, local(): jnp.dot(unit_token_vectors, codebook_matrix.T, precision=TOP_PRECISION)  9.91 us
    all_to_all x1, starting transfers between devices, local(): lax.all_to_all(spaced, 'frames', split_axis=2, concat_axis=1, tiled=True)  7.42 us
    reduce_scatter x1, waiting for transfers between devices, local(): lax.psum_scatter(term_sums, 'frames', scatter_dimension=0, tiled=True)  6.17 us
    reduce_sum x1, other arithmetic, local(): term_counts = jnp.sum(probs, 0)  4.27 us
  transfers between devices with their start and end apart: 3, of which 2 were waited for; matrix products, arithmetic and copies ran while one was open for 25% of the time, Pallas kernels for 0%

commit v1 on v0

--- a/solution.py
+++ b/solution.py
@@ -9,6 +9,18 @@
 DECAY_RATE = 0.9
 EPSILON = 1e-06
 TOP_PRECISION = lax.Precision.HIGHEST
+
+
+def cut_along(x, dim, length):
+    lengths = x.shape
+    pieces = x.reshape(*lengths[:dim], length, lengths[dim] // length, *lengths[dim + 1 :])
+    return jnp.moveaxis(pieces, dim, 0)
+
+
+def in_order(tiles, dim):
+    shape = list(tiles.shape[1:])
+    shape[dim] *= tiles.shape[0]
+    return jnp.moveaxis(tiles, 0, dim).reshape(shape)
 
 
 def rms_norm(values, gain_vec):
@@ -78,7 +90,14 @@
         lambda one_frame: spatial_block(one_frame, gain_space, qkv_space, out_space), flat_frames
     )
     spaced = spaced.reshape(clips, local_frames, places, width)
-    by_place = lax.all_to_all(spaced, "frames", split_axis=2, concat_axis=1, tiled=True)
+    size, here = (lax.axis_size("frames"), lax.axis_index("frames"))
+    parts = cut_along(spaced, 2, size)
+    outs = [parts[here]]
+    for step in range(1, size):
+        sent = parts[(here + step) % size]
+        outs.append(lax.ppermute(sent, "frames", [(i, (i + step) % size) for i in range(size)]))
+    parts = jnp.stack(outs)[(here - jnp.arange(size)) % size]
+    by_place = in_order(parts, 1)
     latents = time_block(by_place, clip_start, gain_time, qkv_time, out_time)
     unit_token_vectors = unit_vec(latents.reshape(-1, width))
     local_codes = unit_vec(code_sums / code_counts[:, None])

time: 200 us -> 191 us (0.955)
  starting transfers between devices: 7.5 us -> 29.4 us
  waiting for transfers between devices: 29.1 us -> 9.02 us
  local copies, waits for them, and re-layouts: 24.8 us -> 13.9 us
    ppermute x0 -> x15, starting transfers between devices: none -> 29.3 us  [local(): lax.ppermute(sent, 'frames', [(i, (i + step) % size) for i in range(size)])]
    all_to_all x1 -> x0, waiting for transfers between devices: 22.8 us -> none  [local(): lax.all_to_all(spaced, 'frames', split_axis=2, concat_axis=1, tiled=True)]
    dynamic_update_slice x4 -> x0, local copies, waits for them, and re-layouts: 13.2 us -> none  [local(): lax.map(lambda one_frame: spatial_block(one_frame, gain_space, qkv_space,...]
    all_to_all x1 -> x0, starting transfers between devices: 7.42 us -> none  [local(): lax.all_to_all(spaced, 'frames', split_axis=2, concat_axis=1, tiled=True)]
    ppermute x0 -> x15, waiting for transfers between devices: none -> 2.58 us  [local(): lax.ppermute(sent, 'frames', [(i, (i + step) % size) for i in range(size)])]
    unnamed x21 -> x36, local copies, waits for them, and re-layouts: 3.85 us -> 4.67 us
  transfers between devices with their start and end apart: 3 -> 17, of which waited for: 2 -> 3; matrix products, arithmetic and copies ran while one was open for 25% -> 21% of each run, Pallas kernels for 0% -> 0%
where the time goes in v1:
time: 191 us; the launch traced here: 190 us
  blocking collectives  63.3 us (33%)
  matrix products  44.3 us (23%)
  starting transfers between devices  29.4 us (15%)
  between operations  15.2 us (8%)
  other arithmetic  14.8 us (8%)
  local copies, waits for them, and re-layouts  13.9 us (7%)
  waiting for transfers between devices  9.02 us (5%)
    unnamed x1, blocking collectives  63.3 us
    ppermute x15, starting transfers between devices, local(): lax.ppermute(sent, 'frames', [(i, (i + step) % size) for i in range(size)])  29.3 us
    dot_general x1, matrix products, local(): lax.dot_general(probs, unit_token_vectors, (((0,), (0,)), ((), ())), prec...  15.1 us
    dot_general x1, matrix products, local(): jnp.dot(unit_token_vectors, codebook_matrix.T, precision=TOP_PRECISION)  9.91 us
    reduce_scatter x1, waiting for transfers between devices, local(): lax.psum_scatter(term_sums, 'frames', scatter_dimension=0, tiled=True)  6.39 us
    unnamed x36, local copies, waits for them, and re-layouts  4.67 us
    reduce_sum x1, other arithmetic, local(): term_counts = jnp.sum(probs, 0)  4.27 us
    dot_general x2, matrix products, spatial_block(): packed = jnp.dot(normed, w_qkv, precision=TOP_PRECISION)  4.17 us
  transfers between devices with their start and end apart: 17, of which 3 were waited for; matrix products, arithmetic and copies ran while one was open for 21% of the time, Pallas kernels for 0%

profile of v1, /device:TPU:0, one launch (start us, length us, event | category | flops | bytes accessed | tf_op | source)
XLA Modules:
  0.0 190.1 jit_solution(1780441460441530563)
XLA Ops:
  8.4 1.8 broadcast_multiply_fusion.2
  10.5 14.1 %while.10 = (s32[]{:T(128)}, f32[2,256,256]{2,1,0:T(8,128)}, f32[2,256,256]{2,1,0:T(8,128)}, f32[256]{0:T(256)}, f32[256,768]{1,0:T(8,128)}, /*index=5*/f32[256,256]{1,0:T(8,128)}, s32[]{:T(128)}) while((s32[]{:T(128)}, f32[2,256,256]{2,1,0:T(8,128)}, f32[2,256,256]{2,1,0:T(8,128)}, f32[256]{0:T(256)}, f32[256,768]{1,0:T(8,128)}, ...), condition=%wide.region_5.6_spmd, body=%wide.region_0.5_spmd.sunk | while | flops 1209269504 | bytes 13154441 | solution.py:89
  11.7 2.1 %fusion.73 = f32[256,768]{1,0:T(8,128)S(1)} fusion(f32[256,768]{1,0:T(8,128)} %get-tuple-element.155, f32[2,256,256]{2,1,0:T(8,128)} %get-tuple-element.153, s32[]{:T(128)} %get-tuple-element.144, f32[256]{0:T(256)} %get-tuple-element.154, f32[256]{0:T(256)S(1)} %add_rsqrt_fusion.10), kind=kOutput, calls=%fused_computation.12.clone.1 | convolution fusion | flops 604110848 | bytes 1837568 | tf_op jit(solution)/shard_map/while/body/eval_jaxpr/dot_general | solution.py:37
  18.7 2.1 %fusion.73 = f32[256,768]{1,0:T(8,128)S(1)} fusion(f32[256,768]{1,0:T(8,128)} %get-tuple-element.155, f32[2,256,256]{2,1,0:T(8,128)} %get-tuple-element.153, s32[]{:T(128)} %get-tuple-element.144, f32[256]{0:T(256)} %get-tuple-element.154, f32[256]{0:T(256)S(1)} %add_rsqrt_fusion.10), kind=kOutput, calls=%fused_computation.12.clone.1 | convolution fusion | flops 604110848 | bytes 1837568 | tf_op jit(solution)/shard_map/while/body/eval_jaxpr/dot_general | solution.py:37
  26.2 2.6 %collective-permute-start.1 = (f32[2,1,16,256]{3,2,0,1:T(8,128)S(1)}, f32[2,1,16,256]{3,2,0,1:T(8,128)S(1)}, u32[]{:S(2)}, u32[]{:S(2)}) collective-permute-start(f32[2,1,16,256]{3,2,0,1:T(8,128)S(1)} %get-tuple-element.74), channel_id=1, source_target_pairs={{0,2},{1,3},{2,4},{3,5},{4,6},{5,7},{6,8},{7,9},{8,10},{9,11},{10,... | collective-permute-start | bytes 98312 | tf_op jit(solution)/shard_map/ppermute | solution.py:98
  28.8 2.4 %collective-permute-start.2 = (f32[2,1,16,256]{3,2,0,1:T(8,128)S(1)}, f32[2,1,16,256]{3,2,0,1:T(8,128)S(1)}, u32[]{:S(2)}, u32[]{:S(2)}) collective-permute-start(f32[2,1,16,256]{3,2,0,1:T(8,128)S(1)} %get-tuple-element.73), channel_id=1, source_target_pairs={{0,3},{1,4},{2,5},{3,6},{4,7},{5,8},{6,9},{7,10},{8,11},{9,12},{10... | collective-permute-start | bytes 98312 | tf_op jit(solution)/shard_map/ppermute | solution.py:98
  35.2 4.3 %collective-permute-start.6 = (f32[2,1,16,256]{3,2,0,1:T(8,128)S(1)}, f32[2,1,16,256]{3,2,0,1:T(8,128)S(1)}, u32[]{:S(2)}, u32[]{:S(2)}) collective-permute-start(f32[2,1,16,256]{3,2,0,1:T(8,128)S(1)} %get-tuple-element.69), channel_id=1, source_target_pairs={{0,7},{1,8},{2,9},{3,10},{4,11},{5,12},{6,13},{7,14},{8,15},{9,0},... | collective-permute-start | bytes 98312 | tf_op jit(solution)/shard_map/ppermute | solution.py:98
  40.2 2.4 %collective-permute-start.9 = (f32[2,1,16,256]{3,2,0,1:T(8,128)S(1)}, f32[2,1,16,256]{3,2,0,1:T(8,128)S(1)}, u32[]{:S(2)}, u32[]{:S(2)}) collective-permute-start(f32[2,1,16,256]{3,2,0,1:T(8,128)S(1)} %get-tuple-element.66), channel_id=1, source_target_pairs={{0,10},{1,11},{2,12},{3,13},{4,14},{5,15},{6,0},{7,1},{8,2},{9,3},... | collective-permute-start | bytes 98312 | tf_op jit(solution)/shard_map/ppermute | solution.py:98
  42.6 2.8 %collective-permute-start.10 = (f32[2,1,16,256]{3,2,0,1:T(8,128)S(1)}, f32[2,1,16,256]{3,2,0,1:T(8,128)S(1)}, u32[]{:S(2)}, u32[]{:S(2)}) collective-permute-start(f32[2,1,16,256]{3,2,0,1:T(8,128)S(1)} %get-tuple-element.65), channel_id=1, source_target_pairs={{0,11},{1,12},{2,13},{3,14},{4,15},{5,0},{6,1},{7,2},{8,3},{9,4},{... | collective-permute-start | bytes 98312 | tf_op jit(solution)/shard_map/ppermute | solution.py:98
  45.5 1.8 collective-permute-start.11
  48.1 4.6 %collective-permute-start.13 = (f32[2,1,16,256]{3,2,0,1:T(8,128)S(1)}, f32[2,1,16,256]{3,2,0,1:T(8,128)S(1)}, u32[]{:S(2)}, u32[]{:S(2)}) collective-permute-start(f32[2,1,16,256]{3,2,0,1:T(8,128)S(1)} %get-tuple-element.62), channel_id=1, source_target_pairs={{0,14},{1,15},{2,0},{3,1},{4,2},{5,3},{6,4},{7,5},{8,6},{9,7},{10,... | collective-permute-start | bytes 98312 | tf_op jit(solution)/shard_map/ppermute | solution.py:98
  52.7 4.1 %collective-permute-start.14 = (f32[2,1,16,256]{3,2,0,1:T(8,128)S(1)}, f32[2,1,16,256]{3,2,0,1:T(8,128)S(1)}, u32[]{:S(2)}, u32[]{:S(2)}) collective-permute-start(f32[2,1,16,256]{3,2,0,1:T(8,128)S(1)} %get-tuple-element.61), channel_id=1, source_target_pairs={{0,15},{1,0},{2,1},{3,2},{4,3},{5,4},{6,5},{7,6},{8,7},{9,8},{10,9... | collective-permute-start | bytes 98312 | tf_op jit(solution)/shard_map/ppermute | solution.py:98
  56.9 1.7 collective-permute-done.14
  64.0 2.5 %reshape.238 = f32[2,16,16,4,64]{4,3,2,1,0:T(4,128)} reshape(f32[2,16,16,256]{3,2,1,0:T(8,128)} %get-tuple-element.58) | data formatting | bytes 1048576 | tf_op jit(solution)/shard_map/reshape | solution.py:55
  69.3 3.1 %fusion.43 = (f32[2,16,4,16]{3,2,1,0:T(4,128)S(1)}, f32[2,16,4,16,16]{3,4,2,1,0:T(8,128)S(1)}) fusion(f32[2,16,16]{1,2,0:T(8,128)S(1)} %and_convert_fusion, f32[2,16,16,4,64]{4,3,2,1,0:T(4,128)S(1)} %get-tuple-element.84, f32[2,16,16,4,64]{4,3,2,1,0:T(4,128)S(1)} %get-tuple-element.85), kind=kOutput, calls=%fused_computation.114 | convolution fusion | flops 25262080 | bytes 1189888 | tf_op jit(solution)/shard_map/ctphd,csphd->cphts/dot_general | solution.py:56
  72.4 2.5 %fusion.18 = f32[2,16,16,4,64]{4,1,3,2,0:T(8,128)S(1)} fusion(f32[2,16,4,16,16]{3,4,2,1,0:T(8,128)S(1)} %get-tuple-element.77, f32[2,16,16,4,64]{4,3,2,1,0:T(4,128)S(1)} %copy-done.6, f32[2,16,16,4]{1,3,2,0:T(4,128)S(1)} %bitcast.215), kind=kOutput, calls=%fused_computation.30 | convolution fusion | flops 25296896 | bytes 1187840 | tf_op jit(solution)/shard_map/cphts,csphd->ctphd/dot_general | solution.py:67
  76.0 1.6 multiply_reduce_fusion.4
  77.9 9.9 %fusion.17 = (f32[512]{0:T(512)S(1)}, f32[512,4096]{1,0:T(8,128)S(1)}) fusion(f32[512,256]{1,0:T(8,128)S(1)} %bitcast_multiply_fusion.2, f32[4096,256]{1,0:T(8,128)} %all-gather.2.cloned.1.call-done), kind=kOutput, calls=%fused_computation.28 | convolution fusion | flops 6446644736 | bytes 13109248 | tf_op jit(solution)/shard_map/dot_general | solution.py:106
  87.8 3.2 %copy-done.1 = f32[512,4096]{1,0:T(8,128)} copy-done((f32[512,4096]{1,0:T(8,128)}, f32[512,4096]{1,0:T(8,128)S(1)}, u32[]{:S(2)}) %copy-start.1) | copy-done | bytes 8388632
  91.1 15.1 %fusion.31 = f32[4096,256]{1,0:T(8,128)} fusion(f32[512,256]{1,0:T(8,128)S(1)} %bitcast_multiply_fusion.2, f32[512,4096]{1,0:T(8,128)S(1)} %get-tuple-element.81, f32[512]{0:T(512)S(1)} %get-tuple-element.80), kind=kOutput, calls=%fused_computation.52 | convolution fusion | flops 6446645248 | bytes 13109248 | tf_op jit(solution)/shard_map/dot_general | solution.py:109
  107.4 4.3 %fusion.30 = f32[4096]{0:T(1024)S(1)} fusion(f32[512]{0:T(512)S(1)} %get-tuple-element.80, f32[512,4096]{1,0:T(8,128)} %copy-done.1), kind=kLoop, calls=%fused_computation.51 | loop fusion | flops 6287360 | bytes 8407040 | tf_op jit(solution)/shard_map/reduce_sum | solution.py:112
  111.7 63.3 %all-reduce = f32[4096]{0:T(1024)S(1)} all-reduce(f32[4096]{0:T(1024)S(1)} %fusion.30), channel_id=3, replica_groups=mesh['groups'=2,'frames'=16] {'frames'}, use_global_device_ids=true, to_apply=%region_15.16.clone | all-reduce | flops 4096 | bytes 32768
  175.1 6.4 %reduce-scatter.2.cloned.1.call-done = f32[256,256]{1,0:T(8,128)} async-done(((f32[4096,256]{1,0:T(8,128)}), f32[256,256]{1,0:T(8,128)}) %reduce-scatter.2.cloned.1.call-update) | async-done | bytes 262160 | tf_op jit(solution)/shard_map/reduce_scatter | solution.py:114
  181.5 1.8 broadcast_divide_fusion
  (121 shorter events, 28.2 us)
Async XLA Ops:
  7.2 52.2 %copy-start = (f32[256,768]{1,0:T(8,128)S(1)}, f32[256,768]{1,0:T(8,128)}, u32[]{:S(2)}) copy-start(f32[256,768]{1,0:T(8,128)} %param.18) | copy-start | bytes 2359300
  7.2 70.7 %all-gather.2.cloned.1.call-start = ((), (), s32[]{:S(2)}) async-start(), calls=%async_computation.1 | async-start | bytes 4456448 | tf_op jit(solution)/shard_map/all_gather | solution.py:104
  10.3 171.2 %reduce-scatter.2.cloned.1.call-start = ((), (), s32[]{:S(2)}) async-start(), calls=%async_computation.2 | async-start | bytes 4456448 | tf_op jit(solution)/shard_map/reduce_scatter | solution.py:114
  10.5 23.3 %copy-start.10 = (s32[2]{0:T(128)S(1)}, s32[2]{0:T(128)}, u32[]{:S(2)}) copy-start(s32[2]{0:T(128)} %param.13) | copy-start | bytes 28
  10.5 48.9 %copy-start.9 = (f32[256]{0:T(256)S(1)}, f32[256]{0:T(256)}, u32[]{:S(2)}) copy-start(f32[256]{0:T(256)} %param.17) | copy-start | bytes 3076
  25.7 8.3 %collective-permute-start = (f32[2,1,16,256]{3,2,0,1:T(8,128)S(1)}, f32[2,1,16,256]{3,2,0,1:T(8,128)S(1)}, u32[]{:S(2)}, u32[]{:S(2)}) collective-permute-start(f32[2,1,16,256]{3,2,0,1:T(8,128)S(1)} %get-tuple-element.75), channel_id=1, source_target_pairs={{0,1},{1,2},{2,3},{3,4},{4,5},{5,6},{6,7},{7,8},{8,9},{9,10},{10,1... | collective-permute-start | bytes 98312 | tf_op jit(solution)/shard_map/ppermute | solution.py:98
  26.2 9.0 %collective-permute-start.1 = (f32[2,1,16,256]{3,2,0,1:T(8,128)S(1)}, f32[2,1,16,256]{3,2,0,1:T(8,128)S(1)}, u32[]{:S(2)}, u32[]{:S(2)}) collective-permute-start(f32[2,1,16,256]{3,2,0,1:T(8,128)S(1)} %get-tuple-element.74), channel_id=1, source_target_pairs={{0,2},{1,3},{2,4},{3,5},{4,6},{5,7},{6,8},{7,9},{8,10},{9,11},{10,... | collective-permute-start | bytes 98312 | tf_op jit(solution)/shard_map/ppermute | solution.py:98
  28.8 10.7 %collective-permute-start.2 = (f32[2,1,16,256]{3,2,0,1:T(8,128)S(1)}, f32[2,1,16,256]{3,2,0,1:T(8,128)S(1)}, u32[]{:S(2)}, u32[]{:S(2)}) collective-permute-start(f32[2,1,16,256]{3,2,0,1:T(8,128)S(1)} %get-tuple-element.73), channel_id=1, source_target_pairs={{0,3},{1,4},{2,5},{3,6},{4,7},{5,8},{6,9},{7,10},{8,11},{9,12},{10... | collective-permute-start | bytes 98312 | tf_op jit(solution)/shard_map/ppermute | solution.py:98
  31.2 8.6 %collective-permute-start.3 = (f32[2,1,16,256]{3,2,0,1:T(8,128)S(1)}, f32[2,1,16,256]{3,2,0,1:T(8,128)S(1)}, u32[]{:S(2)}, u32[]{:S(2)}) collective-permute-start(f32[2,1,16,256]{3,2,0,1:T(8,128)S(1)} %get-tuple-element.72), channel_id=1, source_target_pairs={{0,4},{1,5},{2,6},{3,7},{4,8},{5,9},{6,10},{7,11},{8,12},{9,13},{1... | collective-permute-start | bytes 98312 | tf_op jit(solution)/shard_map/ppermute | solution.py:98
  32.8 7.4 %collective-permute-start.4 = (f32[2,1,16,256]{3,2,0,1:T(8,128)S(1)}, f32[2,1,16,256]{3,2,0,1:T(8,128)S(1)}, u32[]{:S(2)}, u32[]{:S(2)}) collective-permute-start(f32[2,1,16,256]{3,2,0,1:T(8,128)S(1)} %get-tuple-element.71), channel_id=1, source_target_pairs={{0,5},{1,6},{2,7},{3,8},{4,9},{5,10},{6,11},{7,12},{8,13},{9,14},{... | collective-permute-start | bytes 98312 | tf_op jit(solution)/shard_map/ppermute | solution.py:98
  34.0 8.7 %collective-permute-start.5 = (f32[2,1,16,256]{3,2,0,1:T(8,128)S(1)}, f32[2,1,16,256]{3,2,0,1:T(8,128)S(1)}, u32[]{:S(2)}, u32[]{:S(2)}) collective-permute-start(f32[2,1,16,256]{3,2,0,1:T(8,128)S(1)} %get-tuple-element.70), channel_id=1, source_target_pairs={{0,6},{1,7},{2,8},{3,9},{4,10},{5,11},{6,12},{7,13},{8,14},{9,15},... | collective-permute-start | bytes 98312 | tf_op jit(solution)/shard_map/ppermute | solution.py:98
  35.2 10.3 %collective-permute-start.6 = (f32[2,1,16,256]{3,2,0,1:T(8,128)S(1)}, f32[2,1,16,256]{3,2,0,1:T(8,128)S(1)}, u32[]{:S(2)}, u32[]{:S(2)}) collective-permute-start(f32[2,1,16,256]{3,2,0,1:T(8,128)S(1)} %get-tuple-element.69), channel_id=1, source_target_pairs={{0,7},{1,8},{2,9},{3,10},{4,11},{5,12},{6,13},{7,14},{8,15},{9,0},... | collective-permute-start | bytes 98312 | tf_op jit(solution)/shard_map/ppermute | solution.py:98
  39.5 8.6 %collective-permute-start.7 = (f32[2,1,16,256]{3,2,0,1:T(8,128)S(1)}, f32[2,1,16,256]{3,2,0,1:T(8,128)S(1)}, u32[]{:S(2)}, u32[]{:S(2)}) collective-permute-start(f32[2,1,16,256]{3,2,0,1:T(8,128)S(1)} %get-tuple-element.68), channel_id=1, source_target_pairs={{0,8},{1,9},{2,10},{3,11},{4,12},{5,13},{6,14},{7,15},{8,0},{9,1},... | collective-permute-start | bytes 98312 | tf_op jit(solution)/shard_map/ppermute | solution.py:98
  39.9 8.2 %collective-permute-start.8 = (f32[2,1,16,256]{3,2,0,1:T(8,128)S(1)}, f32[2,1,16,256]{3,2,0,1:T(8,128)S(1)}, u32[]{:S(2)}, u32[]{:S(2)}) collective-permute-start(f32[2,1,16,256]{3,2,0,1:T(8,128)S(1)} %get-tuple-element.67), channel_id=1, source_target_pairs={{0,9},{1,10},{2,11},{3,12},{4,13},{5,14},{6,15},{7,0},{8,1},{9,2},... | collective-permute-start | bytes 98312 | tf_op jit(solution)/shard_map/ppermute | solution.py:98
  40.2 12.6 %collective-permute-start.9 = (f32[2,1,16,256]{3,2,0,1:T(8,128)S(1)}, f32[2,1,16,256]{3,2,0,1:T(8,128)S(1)}, u32[]{:S(2)}, u32[]{:S(2)}) collective-permute-start(f32[2,1,16,256]{3,2,0,1:T(8,128)S(1)} %get-tuple-element.66), channel_id=1, source_target_pairs={{0,10},{1,11},{2,12},{3,13},{4,14},{5,15},{6,0},{7,1},{8,2},{9,3},... | collective-permute-start | bytes 98312 | tf_op jit(solution)/shard_map/ppermute | solution.py:98
  42.6 14.2 %collective-permute-start.10 = (f32[2,1,16,256]{3,2,0,1:T(8,128)S(1)}, f32[2,1,16,256]{3,2,0,1:T(8,128)S(1)}, u32[]{:S(2)}, u32[]{:S(2)}) collective-permute-start(f32[2,1,16,256]{3,2,0,1:T(8,128)S(1)} %get-tuple-element.65), channel_id=1, source_target_pairs={{0,11},{1,12},{2,13},{3,14},{4,15},{5,0},{6,1},{7,2},{8,3},{9,4},{... | collective-permute-start | bytes 98312 | tf_op jit(solution)/shard_map/ppermute | solution.py:98
  45.5 11.4 %collective-permute-start.11 = (f32[2,1,16,256]{3,2,0,1:T(8,128)S(1)}, f32[2,1,16,256]{3,2,0,1:T(8,128)S(1)}, u32[]{:S(2)}, u32[]{:S(2)}) collective-permute-start(f32[2,1,16,256]{3,2,0,1:T(8,128)S(1)} %get-tuple-element.64), channel_id=1, source_target_pairs={{0,12},{1,13},{2,14},{3,15},{4,0},{5,1},{6,2},{7,3},{8,4},{9,5},{1... | collective-permute-start | bytes 98312 | tf_op jit(solution)/shard_map/ppermute | solution.py:98
  48.1 8.8 %collective-permute-start.12 = (f32[2,1,16,256]{3,2,0,1:T(8,128)S(1)}, f32[2,1,16,256]{3,2,0,1:T(8,128)S(1)}, u32[]{:S(2)}, u32[]{:S(2)}) collective-permute-start(f32[2,1,16,256]{3,2,0,1:T(8,128)S(1)} %get-tuple-element.63), channel_id=1, source_target_pairs={{0,13},{1,14},{2,15},{3,0},{4,1},{5,2},{6,3},{7,4},{8,5},{9,6},{10... | collective-permute-start | bytes 98312 | tf_op jit(solution)/shard_map/ppermute | solution.py:98
  48.1 8.8 %collective-permute-start.13 = (f32[2,1,16,256]{3,2,0,1:T(8,128)S(1)}, f32[2,1,16,256]{3,2,0,1:T(8,128)S(1)}, u32[]{:S(2)}, u32[]{:S(2)}) collective-permute-start(f32[2,1,16,256]{3,2,0,1:T(8,128)S(1)} %get-tuple-element.62), channel_id=1, source_target_pairs={{0,14},{1,15},{2,0},{3,1},{4,2},{5,3},{6,4},{7,5},{8,6},{9,7},{10,... | collective-permute-start | bytes 98312 | tf_op jit(solution)/shard_map/ppermute | solution.py:98
  52.7 5.9 %collective-permute-start.14 = (f32[2,1,16,256]{3,2,0,1:T(8,128)S(1)}, f32[2,1,16,256]{3,2,0,1:T(8,128)S(1)}, u32[]{:S(2)}, u32[]{:S(2)}) collective-permute-start(f32[2,1,16,256]{3,2,0,1:T(8,128)S(1)} %get-tuple-element.61), channel_id=1, source_target_pairs={{0,15},{1,0},{2,1},{3,2},{4,3},{5,4},{6,5},{7,6},{8,7},{9,8},{10,9... | collective-permute-start | bytes 98312 | tf_op jit(solution)/shard_map/ppermute | solution.py:98
  77.6 28.5 %copy-start.5 = (f32[2,16,16,256]{3,2,1,0:T(8,128)}, f32[2,16,16,256]{3,2,1,0:T(8,128)S(1)}, u32[]{:S(2)}) copy-start(f32[2,16,16,256]{3,2,1,0:T(8,128)S(1)} %get-tuple-element.79) | copy-start | bytes 1572868
  91.1 15.1 %copy-start.11 = (u32[32]{0:T(128)S(1)}, u32[32]{0:T(128)}, u32[]{:S(2)}) copy-start(u32[32]{0:T(128)} %constant.157) | copy-start | bytes 388
  106.1 68.9 %copy-start.7 = (f32[256]{0:T(256)S(1)}, f32[256]{0:T(256)}, u32[]{:S(2)}) copy-start(f32[256]{0:T(256)} %param.21) | copy-start | bytes 3076
  106.1 75.4 %copy-start.4 = (f32[256,256]{1,0:T(8,128)S(1)}, f32[256,256]{1,0:T(8,128)}, u32[]{:S(2)}) copy-start(f32[256,256]{1,0:T(8,128)} %param.20) | copy-start | bytes 786436
  (7 other events, 40.3 us)
Sparse Core Ops, SparseCore 0:
  10.7 58.4 all-gather.1
  106.3 75.1 reduce-scatter.1
